TPU v7x, 32 devices: a whole 2x2x4 slice. The times are simulated.
32 devices in a mesh: dp: 16 (over z, x, core), seq: 2 (over y).
Axes of the slice: x: 2, y: 2, z: 4, core: 2. Of those that a mesh axis runs over, the one named last changes fastest.
Arguments:
- tokens: bfloat16 [16, 1152, 1024], P('dp', 'seq'), may hold values from -6 to 6
- w_qkv: bfloat16 [1024, 3072], P('dp'), may hold values from -0.1875 to 0.1875
- w_out: bfloat16 [1024, 1024], P('dp'), may hold values from -1 to 1
- w_up: bfloat16 [1024, 4096], P('dp'), may hold values from -0.1875 to 0.1875
- w_down: bfloat16 [4096, 1024], P('dp'), may hold values from -0.09375 to 0.09375
- gains: bfloat16 [1024, 2], P('dp'), may hold values from 0.5 to 1.5
- biases: bfloat16 [1024, 6], P('dp'), may hold values from -1.1953125 to 1.1953125
- up_bias: bfloat16 [4096], P('dp'), may hold values from -1.1953125 to 1.1953125
- valid: int32 [16], P('dp'), may hold values from 577 to 1152
- cotangent: bfloat16 [16, 1152, 1024], P('dp', 'seq'), may hold values from -6 to 6
Outputs:
- out_tokens: bfloat16 [16, 1152, 1024], P('dp', 'seq')
- grad_tokens: float32 [16, 1152, 1024], P('dp', 'seq')
- grad_qkv: float32 [1024, 3072], P('dp')
- grad_out: float32 [1024, 1024], P('dp')
- grad_up: float32 [1024, 4096], P('dp')
- grad_down: float32 [4096, 1024], P('dp')
- grad_gains: float32 [1024, 2], P('dp')
- grad_biases: float32 [1024, 6], P('dp')
- grad_up_bias: float32 [4096], P('dp')
Inputs may be any that keep to these rules, and one draw needn't show every extreme that they name: valid counts of the images; keys at positions from valid on are padding.
All inputs are finite; a program needn't handle non-finite values.
Results may differ from a plain program's by a relative error of at most 0.019.
Values may be sent and summed in bfloat16 or wider, within the bound.
A program may use at most 256 MiB of HBM per device.

v0:
```python
import jax
import jax.numpy as jnp
from jax import lax
from jax.sharding import PartitionSpec as P

HD = 64
EPSILON = 1e-06
NEG_FILL = -1e30


def layer_norm(values, scales, offset):
    average = jnp.mean(values, axis=-1, keepdims=True)
    centered = values - average
    variance = jnp.mean(centered * centered, axis=-1, keepdims=True)
    return centered * lax.rsqrt(variance + EPSILON) * scales + offset


def exact_gelu(values):
    return jax.nn.gelu(values, approximate=False)


def split_heads(block):
    seq_len = block.shape[0]
    return block.reshape(seq_len, block.shape[1] // HD, HD)


def score_block(query_heads, key_heads, length):
    scores = jnp.einsum("qhd,khd->hqk", query_heads, key_heads, preferred_element_type=jnp.float32)
    scores = scores * HD ** (-0.5)
    allowed = jnp.arange(key_heads.shape[0], dtype=jnp.int32) < length
    return jnp.where(allowed[None, None, :], scores, NEG_FILL)


def attend_forward(packed):
    queries, keyset, values, length = packed
    query_heads = split_heads(queries)
    key_heads = split_heads(keyset)
    value_heads = split_heads(values)
    scores = score_block(query_heads, key_heads, length)
    row_max = jnp.max(scores, axis=-1, keepdims=True)
    exp_scores = jnp.exp(scores - row_max)
    row_total = jnp.sum(exp_scores, axis=-1, keepdims=True)
    probs = (exp_scores / row_total).astype(jnp.bfloat16)
    result = jnp.einsum("hqk,khd->qhd", probs, value_heads, preferred_element_type=jnp.float32)
    log_total = row_max[..., 0] + jnp.log(row_total[..., 0])
    return (result.reshape(queries.shape).astype(jnp.bfloat16), log_total)


def attend_backward(packed):
    queries, keyset, values, length, log_total, grad_result = packed
    query_heads = split_heads(queries)
    key_heads = split_heads(keyset)
    value_heads = split_heads(values)
    grad_heads = split_heads(grad_result)
    scores = score_block(query_heads, key_heads, length)
    probs = jnp.exp(scores - log_total[:, :, None])
    grad_probs = jnp.einsum(
        "qhd,khd->hqk", grad_heads, value_heads, preferred_element_type=jnp.float32
    )
    row_delta = jnp.sum(probs * grad_probs, axis=-1, keepdims=True)
    grad_scores = (probs * (grad_probs - row_delta)).astype(jnp.bfloat16)
    grad_query = jnp.einsum(
        "hqk,khd->qhd", grad_scores, key_heads, preferred_element_type=jnp.float32
    ) * HD ** (-0.5)
    grad_key = jnp.einsum(
        "hqk,qhd->khd", grad_scores, query_heads, preferred_element_type=jnp.float32
    ) * HD ** (-0.5)
    grad_value = jnp.einsum(
        "hqk,qhd->khd", probs.astype(jnp.bfloat16), grad_heads, preferred_element_type=jnp.float32
    )
    flat_shape = queries.shape
    return (
        grad_query.reshape(flat_shape).astype(jnp.bfloat16),
        grad_key.reshape(flat_shape).astype(jnp.bfloat16),
        grad_value.reshape(flat_shape).astype(jnp.bfloat16),
    )


def per_device(tokens, w_qkv, w_out, w_up, w_down, gains, biases, up_bias, valid, cotangent):
    full_qkv, full_out, full_up, full_down, full_gains, full_biases, full_upb = (
        lax.all_gather(w_qkv, "dp", axis=0, tiled=True),
        lax.all_gather(w_out, "dp", axis=0, tiled=True),
        lax.all_gather(w_up, "dp", axis=0, tiled=True),
        lax.all_gather(w_down, "dp", axis=0, tiled=True),
        lax.all_gather(gains, "dp", axis=0, tiled=True),
        lax.all_gather(biases, "dp", axis=0, tiled=True),
        lax.all_gather(up_bias, "dp", axis=0, tiled=True),
    )
    gain_cols = full_gains.astype(jnp.float32)
    bias_cols = full_biases.astype(jnp.float32)
    upb_float = full_upb.astype(jnp.float32)
    images, local_len, model_width = tokens.shape
    token_shape = (images, local_len, model_width)
    flat_tokens = tokens.reshape(-1, model_width).astype(jnp.float32)
    normed_one, pull_one = jax.vjp(layer_norm, flat_tokens, gain_cols[:, 0], bias_cols[:, 0])
    first = normed_one.astype(jnp.bfloat16)
    mixed = jnp.dot(first, full_qkv, preferred_element_type=jnp.float32)
    queries = (mixed[:, :model_width] + bias_cols[:, 1]).astype(jnp.bfloat16)
    keyset = mixed[:, model_width : 2 * model_width].astype(jnp.bfloat16)
    values = (mixed[:, 2 * model_width :] + bias_cols[:, 2]).astype(jnp.bfloat16)
    head_q, head_k, head_v = (
        lax.all_to_all(
            queries.reshape(token_shape), "seq", split_axis=2, concat_axis=1, tiled=True
        ),
        lax.all_to_all(keyset.reshape(token_shape), "seq", split_axis=2, concat_axis=1, tiled=True),
        lax.all_to_all(values.reshape(token_shape), "seq", split_axis=2, concat_axis=1, tiled=True),
    )
    attended, log_totals = lax.map(attend_forward, (head_q, head_k, head_v, valid))
    back_tokens = lax.all_to_all(attended, "seq", split_axis=1, concat_axis=2, tiled=True)
    merged = back_tokens.reshape(-1, model_width)
    branch = jnp.dot(merged, full_out, preferred_element_type=jnp.float32) + bias_cols[:, 3]
    residual = flat_tokens + branch
    normed_two, pull_two = jax.vjp(layer_norm, residual, gain_cols[:, 1], bias_cols[:, 4])
    second = normed_two.astype(jnp.bfloat16)
    upward = jnp.dot(second, full_up, preferred_element_type=jnp.float32) + upb_float
    activated_float, pull_gelu = jax.vjp(exact_gelu, upward)
    activated = activated_float.astype(jnp.bfloat16)
    output = (
        residual
        + jnp.dot(activated, full_down, preferred_element_type=jnp.float32)
        + bias_cols[:, 5]
    )
    out_tokens = output.astype(jnp.bfloat16).reshape(token_shape)
    back_qkv, back_out, back_up, back_down = (full_qkv, full_out, full_up, full_down)
    grad_output = cotangent.reshape(-1, model_width)
    grad_down = jnp.dot(activated.T, grad_output, preferred_element_type=jnp.float32)
    grad_bias_down = jnp.sum(grad_output.astype(jnp.float32), axis=0)
    grad_act = jnp.dot(grad_output, back_down.T, preferred_element_type=jnp.float32)
    grad_upward = pull_gelu(grad_act)[0].astype(jnp.bfloat16)
    grad_up = jnp.dot(second.T, grad_upward, preferred_element_type=jnp.float32)
    grad_up_bias = jnp.sum(grad_upward.astype(jnp.float32), axis=0)
    grad_second = jnp.dot(grad_upward, back_up.T, preferred_element_type=jnp.float32)
    grad_resid_norm, grad_gain_two, grad_bias_two = pull_two(grad_second)
    grad_resid = grad_output.astype(jnp.float32) + grad_resid_norm
    grad_branch = grad_resid.astype(jnp.bfloat16)
    grad_out_weight = jnp.dot(merged.T, grad_branch, preferred_element_type=jnp.float32)
    grad_bias_out = jnp.sum(grad_branch.astype(jnp.float32), axis=0)
    grad_merged = jnp.dot(grad_branch, back_out.T, preferred_element_type=jnp.float32).astype(
        jnp.bfloat16
    )
    grad_head_result = lax.all_to_all(
        grad_merged.reshape(token_shape), "seq", split_axis=2, concat_axis=1, tiled=True
    )
    grad_q, grad_k, grad_v = lax.map(
        attend_backward, (head_q, head_k, head_v, valid, log_totals, grad_head_result)
    )
    tok_grad_q, tok_grad_k, tok_grad_v = (
        lax.all_to_all(grad_q, "seq", split_axis=1, concat_axis=2, tiled=True),
        lax.all_to_all(grad_k, "seq", split_axis=1, concat_axis=2, tiled=True),
        lax.all_to_all(grad_v, "seq", split_axis=1, concat_axis=2, tiled=True),
    )
    flat_grad_q = tok_grad_q.reshape(-1, model_width)
    flat_grad_v = tok_grad_v.reshape(-1, model_width)
    grad_mixed = jnp.concatenate(
        [flat_grad_q, tok_grad_k.reshape(-1, model_width), flat_grad_v], axis=1
    )
    grad_qkv = jnp.dot(first.T, grad_mixed, preferred_element_type=jnp.float32)
    grad_bias_q = jnp.sum(flat_grad_q.astype(jnp.float32), axis=0)
    grad_bias_v = jnp.sum(flat_grad_v.astype(jnp.float32), axis=0)
    grad_first = jnp.dot(grad_mixed, back_qkv.T, preferred_element_type=jnp.float32)
    grad_tok_norm, grad_gain_one, grad_bias_one = pull_one(grad_first)
    grad_tokens = (grad_resid + grad_tok_norm).reshape(token_shape)
    grad_gains = jnp.stack([grad_gain_one, grad_gain_two], axis=1)
    grad_biases = jnp.stack(
        [grad_bias_one, grad_bias_q, grad_bias_v, grad_bias_out, grad_bias_two, grad_bias_down],
        axis=1,
    )
    piece_qkv, piece_out, piece_up, piece_down, piece_gains, piece_biases, piece_upb = (
        lax.psum_scatter(
            grad_qkv.astype(jnp.bfloat16), "dp", scatter_dimension=0, tiled=True
        ).astype(jnp.float32),
        lax.psum_scatter(
            grad_out_weight.astype(jnp.bfloat16), "dp", scatter_dimension=0, tiled=True
        ).astype(jnp.float32),
        lax.psum_scatter(
            grad_up.astype(jnp.bfloat16), "dp", scatter_dimension=0, tiled=True
        ).astype(jnp.float32),
        lax.psum_scatter(
            grad_down.astype(jnp.bfloat16), "dp", scatter_dimension=0, tiled=True
        ).astype(jnp.float32),
        lax.psum_scatter(
            grad_gains.astype(jnp.bfloat16), "dp", scatter_dimension=0, tiled=True
        ).astype(jnp.float32),
        lax.psum_scatter(
            grad_biases.astype(jnp.bfloat16), "dp", scatter_dimension=0, tiled=True
        ).astype(jnp.float32),
        lax.psum_scatter(
            grad_up_bias.astype(jnp.bfloat16), "dp", scatter_dimension=0, tiled=True
        ).astype(jnp.float32),
    )
    totals = (
        lax.psum(piece_qkv.astype(jnp.bfloat16), "seq").astype(jnp.float32),
        lax.psum(piece_out.astype(jnp.bfloat16), "seq").astype(jnp.float32),
        lax.psum(piece_up.astype(jnp.bfloat16), "seq").astype(jnp.float32),
        lax.psum(piece_down.astype(jnp.bfloat16), "seq").astype(jnp.float32),
        lax.psum(piece_gains.astype(jnp.bfloat16), "seq").astype(jnp.float32),
        lax.psum(piece_biases.astype(jnp.bfloat16), "seq").astype(jnp.float32),
        lax.psum(piece_upb.astype(jnp.bfloat16), "seq").astype(jnp.float32),
    )
    return (
        out_tokens,
        grad_tokens,
        totals[0],
        totals[1],
        totals[2],
        totals[3],
        totals[4],
        totals[5],
        totals[6],
    )


def solution(mesh):
    return jax.shard_map(
        per_device,
        mesh=mesh,
        in_specs=(
            P("dp", "seq", None),
            P("dp", None),
            P("dp", None),
            P("dp", None),
            P("dp", None),
            P("dp", None),
            P("dp", None),
            P("dp"),
            P("dp"),
            P("dp", "seq", None),
        ),
        out_specs=(
            P("dp", "seq", None),
            P("dp", "seq", None),
            P("dp", None),
            P("dp", None),
            P("dp", None),
            P("dp", None),
            P("dp", None),
            P("dp", None),
            P("dp"),
        ),
        check_vma=False,
    )
```

profile of v0, /device:TPU:0, one launch (start us, length us, event | category | flops | bytes accessed | tf_op | source)
XLA Modules:
  0.0 1100.0 jit_solution(14046963542723650582)
XLA Ops:
  9.4 23.2 %all-gather = bf16[16,64,2]{1,2,0:T(2,128)(2,1)S(1)} all-gather(bf16[1,64,2]{1,2,0:T(2,128)(2,1)} %bitcast.251), channel_id=1, replica_groups=mesh['dp'=16,'seq'=2] {'dp'}, dimensions={0}, use_global_device_ids=true | all-gather | bytes 4352 | tf_op jit(solution)/shard_map/all_gather | solution.py:85
  32.7 17.9 %all-gather.1 = bf16[16,64,6]{1,2,0:T(8,128)(2,1)S(1)} all-gather(bf16[1,64,6]{1,2,0:T(8,128)(2,1)} %bitcast.250), channel_id=1, replica_groups=mesh['dp'=16,'seq'=2] {'dp'}, dimensions={0}, use_global_device_ids=true | all-gather | bytes 13056 | tf_op jit(solution)/shard_map/all_gather | solution.py:86
  53.4 21.5 %all-gather.8.cloned.1.call-done = bf16[1024,3072]{1,0:T(8,128)(2,1)} async-done(((bf16[64,3072]{1,0:T(8,128)(2,1)}), bf16[1024,3072]{1,0:T(8,128)(2,1)}) %all-gather.8.cloned.1.call-update) | async-done | bytes 6291472 | tf_op jit(solution)/shard_map/all_gather | solution.py:81
  208.8 16.1 %fusion.59 = (f32[8,1152]{1,0:T(8,128)S(1)}, f32[8,1152,1152]{1,2,0:T(8,128)}) fusion(bf16[1152,8,64]{0,2,1:T(8,128)(2,1)S(1)} %reshape.230, bf16[1152,8,64]{0,2,1:T(8,128)(2,1)S(1)} %reshape.232, pred[1152]{0:T(1024)(128)(4,1)S(1)} %iota_compare_fusion), kind=kOutput, calls=%fused_computation.104 | convolution fusion | flops 1390795776 | bytes 44864640 | tf_op jit(solution)/shard_map/while/body/eval_jaxpr/qhd,khd->hqk/dot_general | solution.py:28
  224.9 17.4 %fusion.1 = f32[8,1152]{1,0:T(8,128)S(1)} fusion(f32[8,1152,1152]{1,2,0:T(8,128)} %get-tuple-element.91, f32[8,1152]{1,0:T(8,128)S(1)} %get-tuple-element.90), kind=kLoop, calls=%fused_computation.7 | loop fusion | flops 21224448 | bytes 42541056 | tf_op jit(solution)/shard_map/while/body/eval_jaxpr/reduce_sum | solution.py:42
  242.4 18.1 %fusion.18 = bf16[8,64,1152]{2,1,0:T(8,128)(2,1)} fusion(bf16[1152,8,64]{0,2,1:T(8,128)(2,1)S(1)} %copy-done.17, f32[8,1152,1152]{1,2,0:T(8,128)} %get-tuple-element.91, f32[8,1152]{1,0:T(8,128)S(1)} %fusion.1, f32[8,1152]{1,0:T(8,128)S(1)} %get-tuple-element.90), kind=kOutput, calls=%fused_computation.39 | convolution fusion | flops 1391394816 | bytes 44900352 | tf_op jit(solution)/shard_map/while/body/eval_jaxpr/hqk,khd->qhd/dot_general | solution.py:44
  282.6 18.8 %all-gather.2 = bf16[16,1,256]{2,1,0:T(2,128)(2,1)S(1)} all-gather(bf16[1,1,256]{2,1,0:T(2,128)(2,1)S(1)} %reshape.246), channel_id=1, replica_groups=mesh['dp'=16,'seq'=2] {'dp'}, dimensions={0}, use_global_device_ids=true | all-gather | bytes 8704 | tf_op jit(solution)/shard_map/all_gather | solution.py:87
  310.8 30.8 %multiply_convert_fusion.1 = (bf16[576,4096]{1,0:T(8,128)(2,1)}, f32[576,4096]{1,0:T(8,128)}, f32[576,4096]{1,0:T(8,128)}) fusion(f32[4096]{0:T(1024)} %bitcast.240, bf16[1024,4096]{1,0:T(8,128)(2,1)} %all-gather.12.cloned.1.call-done, f32[576,1024]{1,0:T(8,128)S(1)} %get-tuple-element.93, f32[1024]{0:T(1024)} %bitcast.245, f32[1024]{0:T(1024)S(1)} %bitcast.234, ...), kind=kOutput, calls=%fused_computation.15 | convolution fusion | flops 4990500864 | bytes 34370048 | tf_op jit(solution)/shard_map/dot_general | solution.py:115
  341.7 15.7 %fusion.61 = (bf16[4096]{0:T(1024)(128)(2,1)}, bf16[576,4096]{1,0:T(8,128)(2,1)S(1)}) fusion(f32[576,4096]{1,0:T(8,128)} %get-tuple-element.79, bf16[4096,1024]{1,0:T(8,128)(2,1)} %all-gather.14.cloned.1.call-done, bf16[1,576,1024]{2,1,0:T(8,128)(2,1)S(1)} %copy-done.8, f32[576,4096]{1,0:T(8,128)} %get-tuple-element.94, f32[4096]{0:T(1024)} %bitcast.241), kind=kOutput, calls=%fused_computation.106 | convolution fusion | flops 4869582848 | bytes 33185792 | tf_op jit(solution)/shard_map/dot_general | solution.py:128
  357.4 10.7 multiply_reduce_fusion.1
  401.2 12.2 %all-to-all-done.4 = bf16[2,2,147456]{2,1,0:T(2,128)(2,1)} async-done(((bf16[2,2,147456]{2,1,0:T(2,128)(2,1)}), bf16[2,2,147456]{2,1,0:T(2,128)(2,1)}, u32[]{:S(2)}, u32[]{:S(2)}) %all-to-all-start.4) | async-done | bytes 1179680 | tf_op jit(solution)/shard_map/all_to_all | solution.py:141
  425.4 16.5 %fusion.15 = bf16[8,64,1152]{2,1,0:T(8,128)(2,1)S(1)} fusion(bf16[1152,8,64]{0,2,1:T(8,128)(2,1)S(1)} %reshape.237, f32[8,1152,1152]{1,2,0:T(8,128)} %get-tuple-element.91, f32[8,1152]{1,0:T(8,128)} %log_add_fusion), kind=kOutput, calls=%fused_computation.38 | convolution fusion | flops 1380777984 | bytes 44863488 | tf_op jit(solution)/shard_map/while/body/eval_jaxpr/hqk,qhd->khd/dot_general | solution.py:68
  442.0 32.1 %multiply_reduce_fusion = (f32[8,1152]{1,0:T(8,128)}, f32[8,1152,1152]{1,2,0:T(8,128)}) fusion(f32[8,1152,1152]{1,2,0:T(8,128)} %get-tuple-element.91, f32[8,1152]{1,0:T(8,128)} %log_add_fusion, bf16[1152,8,64]{0,2,1:T(8,128)(2,1)S(1)} %reshape.237, bf16[1152,8,64]{0,2,1:T(8,128)(2,1)S(1)} %copy-done.18), kind=kOutput, calls=%fused_computation.3 | convolution fusion | flops 1390795776 | bytes 87367680 | tf_op jit(solution)/shard_map/while/body/eval_jaxpr/qhd,khd->hqk/dot_general | solution.py:57
  492.1 34.8 %multiply_convert_fusion = bf16[8,1152,1152]{1,2,0:T(8,128)(2,1)} fusion(f32[8,1152,1152]{1,2,0:T(8,128)} %get-tuple-element.97, f32[8,1152,1152]{1,2,0:T(8,128)} %get-tuple-element.91, f32[8,1152]{1,0:T(8,128)S(1)} %copy-done.27, f32[8,1152]{1,0:T(8,128)S(1)} %copy-done.19), kind=kLoop, calls=%fused_computation.2 | loop fusion | flops 42467328 | bytes 106242048 | tf_op jit(solution)/shard_map/while/body/eval_jaxpr/convert_element_type | solution.py:61
  526.9 10.7 fusion.14
  555.7 10.5 fusion.13
  615.3 12.2 %convolution_convert_fusion = bf16[1024,4096]{1,0:T(8,128)(2,1)} fusion(bf16[576,4096]{1,0:T(8,128)(2,1)} %copy-done.49, f32[576,1024]{1,0:T(8,128)} %copy-done.10, f32[1024]{0:T(1024)} %bitcast.246, f32[1024]{0:T(1024)} %bitcast.237, f32[576]{0:T(1024)} %copy-done.40, f32[576]{0:T(1024)S(1)} %broadcast_multiply_fusion), kind=kOutput, calls=%fused_computation.29 | convolution fusion | flops 4838981632 | bytes 15479296 | tf_op jit(solution)/shard_map/dot_general | solution.py:130
  627.6 11.2 %convolution_convert_fusion.1 = bf16[4096,1024]{1,0:T(8,128)(2,1)} fusion(bf16[576,4096]{1,0:T(8,128)(2,1)} %get-tuple-element.78, bf16[1,576,1024]{2,1,0:T(8,128)(2,1)} %param.19), kind=kOutput, calls=%fused_computation.30 | convolution fusion | flops 4836032512 | bytes 14286848 | tf_op jit(solution)/shard_map/dot_general | solution.py:126
  664.7 31.7 %all-reduce = bf16[4096]{0:T(1024)(128)(2,1)S(1)} all-reduce(bf16[4096]{0:T(1024)(128)(2,1)} %get-tuple-element.99), channel_id=8, replica_groups=mesh['dp'=16,'seq'=2] {'dp'}, use_global_device_ids=true, to_apply=%region_32.33.clone | all-reduce | flops 4096 | bytes 16384
  698.9 107.8 %reduce-scatter.15.cloned.1.call-done = bf16[64,4096]{1,0:T(8,128)(2,1)} async-done(((bf16[1024,4096]{1,0:T(8,128)(2,1)}), bf16[64,4096]{1,0:T(8,128)(2,1)}) %reduce-scatter.15.cloned.1.call-update) | async-done | bytes 524304 | tf_op jit(solution)/shard_map/reduce_scatter | solution.py:175
  806.6 108.5 %reduce-scatter.17.cloned.1.call-done = bf16[256,1024]{1,0:T(8,128)(2,1)} async-done(((bf16[4096,1024]{1,0:T(8,128)(2,1)}), bf16[256,1024]{1,0:T(8,128)(2,1)}) %reduce-scatter.17.cloned.1.call-update) | async-done | bytes 524304 | tf_op jit(solution)/shard_map/reduce_scatter | solution.py:178
  927.9 46.4 %reduce-scatter.19.cloned.1.call-done = bf16[64,2]{1,0:T(8,128)(2,1)} async-done(((bf16[1024,2]{1,0:T(8,128)(2,1)}), bf16[64,2]{1,0:T(8,128)(2,1)}) %reduce-scatter.19.cloned.1.call-update) | async-done | bytes 272
  975.1 57.5 %reduce-scatter.21.cloned.1.call-done = bf16[64,6]{1,0:T(8,128)(2,1)} async-done(((bf16[1024,6]{1,0:T(8,128)(2,1)}), bf16[64,6]{1,0:T(8,128)(2,1)}) %reduce-scatter.21.cloned.1.call-update) | async-done | bytes 784
  1040.0 46.1 %all-reduce.5.cloned.1.call-done = (bf16[64,3072]{1,0:T(8,128)(2,1)}, bf16[64,1024]{1,0:T(8,128)(2,1)}, bf16[64,4096]{1,0:T(8,128)(2,1)}, bf16[256,1024]{1,0:T(8,128)(2,1)}) async-done(((bf16[64,3072]{1,0:T(8,128)(2,1)}, bf16[64,1024]{1,0:T(8,128)(2,1)}, bf16[64,4096]{1,0:T(8,128)(2,1)}, bf16[256,1024]{1,0:T(8,128)(2,1)}), (bf16[64,3072]{1,0:T(8,128)(2,1)}, bf16[64,1024]{1,0:T(8,128)(2,1)}, ...) | async-done | bytes 1572880 | tf_op jit(solution)/shard_map/psum | solution.py:192
  (267 shorter events, 355.1 us)
Async XLA Ops:
  7.2 45.0 %copy-start.2 = (bf16[1,576,1024]{2,1,0:T(8,128)(2,1)S(1)}, bf16[1,576,1024]{2,1,0:T(8,128)(2,1)}, u32[]{:S(2)}) copy-start(bf16[1,576,1024]{2,1,0:T(8,128)(2,1)} %param.10) | copy-start | bytes 3538948
  7.2 67.7 %all-gather.8.cloned.1.call-start = ((), (), s32[]{:S(2)}) async-start(), calls=%async_computation.14 | async-start | bytes 6684672 | tf_op jit(solution)/shard_map/all_gather | solution.py:81
  7.9 299.0 %all-gather.10.cloned.1.call-start = ((), (), s32[]{:S(2)}) async-start(), calls=%async_computation.15 | async-start | bytes 2228224 | tf_op jit(solution)/shard_map/all_gather | solution.py:82
  8.7 302.1 %all-gather.12.cloned.1.call-start = ((), (), s32[]{:S(2)}) async-start(), calls=%async_computation.16 | async-start | bytes 8912896 | tf_op jit(solution)/shard_map/all_gather | solution.py:83
  52.7 315.3 %copy-start.41 = (f32[1024,1]{0,1:T(1,128)}, f32[1024,1]{0,1:T(1,128)S(1)}, u32[]{:S(2)}) copy-start(f32[1024,1]{0,1:T(1,128)S(1)} %get-tuple-element.88) | copy-start | bytes 12292
  101.3 23.0 %all-to-all-start.1 = ((bf16[2,2,147456]{2,1,0:T(2,128)(2,1)}), bf16[2,2,147456]{2,1,0:T(2,128)(2,1)}, u32[]{:S(2)}, u32[]{:S(2)}) async-start(bf16[2,2,147456]{2,1,0:T(2,128)(2,1)} %reshape.262), calls=%async_computation.1 | async-start | bytes 2359296 | tf_op jit(solution)/shard_map/all_to_all | solution.py:102
  124.3 21.5 %all-to-all-start.2 = ((bf16[2,2,147456]{2,1,0:T(2,128)(2,1)}), bf16[2,2,147456]{2,1,0:T(2,128)(2,1)}, u32[]{:S(2)}, u32[]{:S(2)}) async-start(bf16[2,2,147456]{2,1,0:T(2,128)(2,1)} %reshape.264), calls=%async_computation.2 | async-start | bytes 2359296 | tf_op jit(solution)/shard_map/all_to_all | solution.py:105
  145.8 41.7 %all-to-all-start = ((bf16[2,2,147456]{2,1,0:T(2,128)(2,1)}), bf16[2,2,147456]{2,1,0:T(2,128)(2,1)}, u32[]{:S(2)}, u32[]{:S(2)}) async-start(bf16[2,2,147456]{2,1,0:T(2,128)(2,1)} %reshape.260), calls=%async_computation | async-start | bytes 2359296 | tf_op jit(solution)/shard_map/all_to_all | solution.py:106
  150.3 191.4 %all-gather.14.cloned.1.call-start = ((), (), s32[]{:S(2)}) async-start(), calls=%async_computation.17 | async-start | bytes 8912896 | tf_op jit(solution)/shard_map/all_gather | solution.py:84
  278.1 23.9 %all-to-all-start.3 = ((bf16[2,2,147456]{2,1,0:T(2,128)(2,1)}), bf16[2,2,147456]{2,1,0:T(2,128)(2,1)}, u32[]{:S(2)}, u32[]{:S(2)}) async-start(bf16[2,2,147456]{2,1,0:T(2,128)(2,1)} %reshape.266), calls=%async_computation.3 | async-start | bytes 2359296 | tf_op jit(solution)/shard_map/all_to_all | solution.py:109
  310.4 57.7 %copy-start.10 = (f32[576,1024]{1,0:T(8,128)}, f32[576,1024]{1,0:T(8,128)S(1)}, u32[]{:S(2)}) copy-start(f32[576,1024]{1,0:T(8,128)S(1)} %get-tuple-element.93) | copy-start | bytes 7077892
  310.8 57.3 %copy-start.40 = (f32[576]{0:T(1024)}, f32[576]{0:T(1024)S(1)}, u32[]{:S(2)}) copy-start(f32[576]{0:T(1024)S(1)} %fusion.46) | copy-start | bytes 6916
  392.8 20.6 %all-to-all-start.4 = ((bf16[2,2,147456]{2,1,0:T(2,128)(2,1)}), bf16[2,2,147456]{2,1,0:T(2,128)(2,1)}, u32[]{:S(2)}, u32[]{:S(2)}) async-start(bf16[2,2,147456]{2,1,0:T(2,128)(2,1)} %reshape.268), calls=%async_computation.4 | async-start | bytes 2359296 | tf_op jit(solution)/shard_map/all_to_all | solution.py:141
  397.3 299.1 %reduce-scatter.13.cloned.1.call-start = ((), (), s32[]{:S(2)}) async-start(), calls=%async_computation.19 | async-start | bytes 2228224 | tf_op jit(solution)/shard_map/reduce_scatter | solution.py:172
  487.6 63.7 %all-to-all-start.7 = ((bf16[2,2,147456]{2,1,0:T(2,128)(2,1)}), bf16[2,2,147456]{2,1,0:T(2,128)(2,1)}, u32[]{:S(2)}, u32[]{:S(2)}) async-start(bf16[2,2,147456]{2,1,0:T(2,128)(2,1)} %reshape.274), calls=%async_computation.7 | async-start | bytes 2359296 | tf_op jit(solution)/shard_map/all_to_all | solution.py:150
  551.2 28.5 %all-to-all-start.6 = ((bf16[2,2,147456]{2,1,0:T(2,128)(2,1)}), bf16[2,2,147456]{2,1,0:T(2,128)(2,1)}, u32[]{:S(2)}, u32[]{:S(2)}) async-start(bf16[2,2,147456]{2,1,0:T(2,128)(2,1)} %reshape.272), calls=%async_computation.6 | async-start | bytes 2359296 | tf_op jit(solution)/shard_map/all_to_all | solution.py:149
  579.8 19.1 %all-to-all-start.5 = ((bf16[2,2,147456]{2,1,0:T(2,128)(2,1)}), bf16[2,2,147456]{2,1,0:T(2,128)(2,1)S(1)}, u32[]{:S(2)}, u32[]{:S(2)}) async-start(bf16[2,2,147456]{2,1,0:T(2,128)(2,1)} %reshape.270), calls=%async_computation.5 | async-start | bytes 2359296 | tf_op jit(solution)/shard_map/all_to_all | solution.py:148
  583.4 115.5 %reduce-scatter.11.cloned.1.call-start = ((), (), s32[]{:S(2)}) async-start(), calls=%async_computation.18 | async-start | bytes 6684672 | tf_op jit(solution)/shard_map/reduce_scatter | solution.py:169
  615.3 191.4 %reduce-scatter.15.cloned.1.call-start = ((), (), s32[]{:S(2)}) async-start(), calls=%async_computation.20 | async-start | bytes 8912896 | tf_op jit(solution)/shard_map/reduce_scatter | solution.py:175
  627.5 287.6 %reduce-scatter.17.cloned.1.call-start = ((), (), s32[]{:S(2)}) async-start(), calls=%async_computation.21 | async-start | bytes 8912896 | tf_op jit(solution)/shard_map/reduce_scatter | solution.py:178
  638.8 335.5 %reduce-scatter.19.cloned.1.call-start = ((), (), s32[]{:S(2)}) async-start(), calls=%async_computation.22 | async-start | bytes 278528
  652.7 379.9 %reduce-scatter.21.cloned.1.call-start = ((), (), s32[]{:S(2)}) async-start(), calls=%async_computation.23 | async-start | bytes 278528
  659.5 255.7 %copy-start.43 = (f32[1024,1]{0,1:T(1,128)S(1)}, f32[1024,1]{0,1:T(1,128)}, u32[]{:S(2)}) copy-start(f32[1024,1]{0,1:T(1,128)} %get-tuple-element.82) | copy-start | bytes 12292
  662.7 423.5 %all-reduce.5.cloned.1.call-start = ((), (), s32[]{:S(2)}) async-start(), calls=%async_computation.24 | async-start | bytes 3145728 | tf_op jit(solution)/shard_map/psum | solution.py:192
  (45 other events, 507.2 us)
Sparse Core Ops, SparseCore 0:
  10.3 64.5 all-gather.7
  77.1 40.0 all-gather.9
  119.4 73.6 all-gather.11
  195.1 73.1 all-gather.13
  401.6 59.3 reduce-scatter.12
  615.4 83.4 reduce-scatter.10
  702.9 103.6 reduce-scatter.14
  810.7 104.3 reduce-scatter.16
  919.2 55.0 reduce-scatter.18
  978.2 54.3 reduce-scatter.20
  1035.1 51.0 all-reduce.4
where the time goes:
time: 1110 us; the launch traced here: 1100 us
  waiting for transfers between devices  405 us (36%)
  matrix products  226 us (20%)
  local copies, waits for them, and re-layouts  173 us (16%)
  other arithmetic  147 us (13%)
  blocking collectives  96.4 us (9%)
  starting transfers between devices  35.5 us (3%)
  between operations  16.6 us (1%)
    reduce_scatter x1, waiting for transfers between devices, per_device(): lax.psum_scatter(grad_down.astype(jnp.bfloat16), 'dp', scatter_dimension=...  108 us
    reduce_scatter x1, waiting for transfers between devices, per_device(): lax.psum_scatter(grad_up.astype(jnp.bfloat16), 'dp', scatter_dimension=0,...  108 us
    unnamed x13, waiting for transfers between devices  107 us
    unnamed x140, local copies, waits for them, and re-layouts  80.5 us
    unnamed x8, other arithmetic  71.4 us
    psum x1, waiting for transfers between devices, per_device(): lax.psum(piece_qkv.astype(jnp.bfloat16), 'seq').astype(jnp.float32)  46.1 us
    convert_element_type x1, other arithmetic, attend_backward(): grad_scores = (probs * (grad_probs - row_delta)).astype(jnp.bfloat16)  34.8 us
    dot_general x1, matrix products, attend_backward(): jnp.einsum('qhd,khd->hqk', grad_heads, value_heads, preferred_element_typ...  32.1 us
  transfers between devices with their start and end apart: 19, of which 8 were waited for; matrix products, arithmetic and copies ran while one was open for 44% of the time, Pallas kernels for 0%

commit v1 on v0

--- a/solution.py
+++ b/solution.py
@@ -189,7 +189,7 @@
         ).astype(jnp.float32),
     )
     totals = (
-        lax.psum(piece_qkv.astype(jnp.bfloat16), "seq").astype(jnp.float32),
+        jnp.sum(lax.all_gather(piece_qkv.astype(jnp.bfloat16), "seq"), axis=0).astype(jnp.float32),
         lax.psum(piece_out.astype(jnp.bfloat16), "seq").astype(jnp.float32),
         lax.psum(piece_up.astype(jnp.bfloat16), "seq").astype(jnp.float32),
         lax.psum(piece_down.astype(jnp.bfloat16), "seq").astype(jnp.float32),

time: 1110 us -> 930 us (0.84)
  waiting for transfers between devices: 405 us -> 201 us
  blocking collectives: 96.4 us -> 111 us
    reduce_scatter x1, waiting for transfers between devices: 108 us -> 0.02 us  [per_device(): lax.psum_scatter(grad_down.astype(jnp.bfloat16), 'dp', scatter_dimension=...]
    reduce_scatter x1, waiting for transfers between devices: 108 us -> 0.02 us  [per_device(): lax.psum_scatter(grad_up.astype(jnp.bfloat16), 'dp', scatter_dimension=0,...]
    reduce_scatter x1, waiting for transfers between devices: 2.48 us -> 81 us  [per_device(): lax.psum_scatter(grad_qkv.astype(jnp.bfloat16), 'dp', scatter_dimension=0...]
    unnamed x13, waiting for transfers between devices: 107 us -> 63.7 us
    psum x1, waiting for transfers between devices: 46.1 us -> 30.4 us  [per_device(): lax.psum(piece_out.astype(jnp.bfloat16), 'seq').astype(jnp.float32)]
    all_gather x0 -> x1, blocking collectives: none -> 15.1 us  [per_device(): lax.all_gather(piece_qkv.astype(jnp.bfloat16), 'seq')]
    unnamed x140 -> x128, local copies, waits for them, and re-layouts: 80.5 us -> 79 us
  transfers between devices with their start and end apart: 19 -> 19, of which waited for: 8 -> 6; matrix products, arithmetic and copies ran while one was open for 44% -> 55% of each run, Pallas kernels for 0% -> 0%
where the time goes in v1:
time: 930 us; the launch traced here: 918 us
  matrix products  232 us (25%)
  waiting for transfers between devices  201 us (22%)
  local copies, waits for them, and re-layouts  171 us (18%)
  other arithmetic  150 us (16%)
  blocking collectives  111 us (12%)
  starting transfers between devices  35.5 us (4%)
  between operations  16.5 us (2%)
    reduce_scatter x1, waiting for transfers between devices, per_device(): lax.psum_scatter(grad_qkv.astype(jnp.bfloat16), 'dp', scatter_dimension=0...  81 us
    unnamed x128, local copies, waits for them, and re-layouts  79 us
    unnamed x8, other arithmetic  71.4 us
    unnamed x13, waiting for transfers between devices  63.7 us
    convert_element_type x1, other arithmetic, attend_backward(): grad_scores = (probs * (grad_probs - row_delta)).astype(jnp.bfloat16)  35.3 us
    dot_general x1, matrix products, attend_backward(): jnp.einsum('qhd,khd->hqk', grad_heads, value_heads, preferred_element_typ...  32.3 us
    unnamed x1, blocking collectives  30.8 us
    dot_general x1, matrix products, per_device(): jnp.dot(second, full_up, preferred_element_type=jnp.float32) + upb_float  30.8 us
  transfers between devices with their start and end apart: 19, of which 6 were waited for; matrix products, arithmetic and copies ran while one was open for 55% of the time, Pallas kernels for 0%

profile of v1, /device:TPU:0, one launch (start us, length us, event | category | flops | bytes accessed | tf_op | source)
XLA Modules:
  0.0 917.7 jit_solution(10595692683986448928)
XLA Ops:
  9.4 23.2 %all-gather.1 = bf16[16,64,2]{1,2,0:T(2,128)(2,1)S(1)} all-gather(bf16[1,64,2]{1,2,0:T(2,128)(2,1)} %bitcast.253), channel_id=1, replica_groups=mesh['dp'=16,'seq'=2] {'dp'}, dimensions={0}, use_global_device_ids=true | all-gather | bytes 4352 | tf_op jit(solution)/shard_map/all_gather | solution.py:85
  32.7 17.9 %all-gather.2 = bf16[16,64,6]{1,2,0:T(8,128)(2,1)S(1)} all-gather(bf16[1,64,6]{1,2,0:T(8,128)(2,1)} %bitcast.252), channel_id=1, replica_groups=mesh['dp'=16,'seq'=2] {'dp'}, dimensions={0}, use_global_device_ids=true | all-gather | bytes 13056 | tf_op jit(solution)/shard_map/all_gather | solution.py:86
  53.4 21.5 %all-gather.9.cloned.1.call-done = bf16[1024,3072]{1,0:T(8,128)(2,1)} async-done(((bf16[64,3072]{1,0:T(8,128)(2,1)}), bf16[1024,3072]{1,0:T(8,128)(2,1)}) %all-gather.9.cloned.1.call-update) | async-done | bytes 6291472 | tf_op jit(solution)/shard_map/all_gather | solution.py:81
  112.0 10.0 %reduce.13 = bf16[1024,576]{1,0:T(8,128)(2,1)S(1)} reduce(bf16[1024,1,576]{2,1,0:T(2,128)(2,1)} %bitcast.190, bf16[]{:T(256)} %broadcast.145), dimensions={1}, to_apply=%bitcast.141.reduce_sub_computation | reduce | bytes 2359298
  208.8 16.0 %fusion.59 = (f32[8,1152]{1,0:T(8,128)S(1)}, f32[8,1152,1152]{1,2,0:T(8,128)}) fusion(bf16[1152,8,64]{0,2,1:T(8,128)(2,1)S(1)} %reshape.230, bf16[1152,8,64]{0,2,1:T(8,128)(2,1)S(1)} %reshape.232, pred[1152]{0:T(1024)(128)(4,1)S(1)} %iota_compare_fusion), kind=kOutput, calls=%fused_computation.104 | convolution fusion | flops 1390795776 | bytes 44864640 | tf_op jit(solution)/shard_map/while/body/eval_jaxpr/qhd,khd->hqk/dot_general | solution.py:28
  224.8 17.4 %fusion.1 = f32[8,1152]{1,0:T(8,128)S(1)} fusion(f32[8,1152,1152]{1,2,0:T(8,128)} %get-tuple-element.90, f32[8,1152]{1,0:T(8,128)S(1)} %get-tuple-element.89), kind=kLoop, calls=%fused_computation.7 | loop fusion | flops 21224448 | bytes 42541056 | tf_op jit(solution)/shard_map/while/body/eval_jaxpr/reduce_sum | solution.py:42
  242.3 18.1 %fusion.18 = bf16[8,64,1152]{2,1,0:T(8,128)(2,1)} fusion(bf16[1152,8,64]{0,2,1:T(8,128)(2,1)S(1)} %copy-done.15, f32[8,1152,1152]{1,2,0:T(8,128)} %get-tuple-element.90, f32[8,1152]{1,0:T(8,128)S(1)} %fusion.1, f32[8,1152]{1,0:T(8,128)S(1)} %get-tuple-element.89), kind=kOutput, calls=%fused_computation.39 | convolution fusion | flops 1391394816 | bytes 44900352 | tf_op jit(solution)/shard_map/while/body/eval_jaxpr/hqk,khd->qhd/dot_general | solution.py:44
  282.4 19.0 %all-gather.3 = bf16[16,1,256]{2,1,0:T(2,128)(2,1)S(1)} all-gather(bf16[1,1,256]{2,1,0:T(2,128)(2,1)S(1)} %reshape.247), channel_id=1, replica_groups=mesh['dp'=16,'seq'=2] {'dp'}, dimensions={0}, use_global_device_ids=true | all-gather | bytes 8704 | tf_op jit(solution)/shard_map/all_gather | solution.py:87
  310.9 30.8 %multiply_convert_fusion.1 = (bf16[576,4096]{1,0:T(8,128)(2,1)}, f32[576,4096]{1,0:T(8,128)}, f32[576,4096]{1,0:T(8,128)}) fusion(f32[4096]{0:T(1024)} %bitcast.242, bf16[1024,4096]{1,0:T(8,128)(2,1)} %all-gather.13.cloned.1.call-done, f32[576,1024]{1,0:T(8,128)S(1)} %get-tuple-element.92, f32[1024]{0:T(1024)} %bitcast.249, f32[1024]{0:T(1024)S(1)} %bitcast.236, ...), kind=kOutput, calls=%fused_computation.15 | convolution fusion | flops 4990500864 | bytes 34370048 | tf_op jit(solution)/shard_map/dot_general | solution.py:115
  341.7 15.6 %fusion.61 = (bf16[4096]{0:T(1024)(128)(2,1)}, bf16[576,4096]{1,0:T(8,128)(2,1)S(1)}) fusion(f32[576,4096]{1,0:T(8,128)} %get-tuple-element.78, bf16[4096,1024]{1,0:T(8,128)(2,1)} %all-gather.15.cloned.1.call-done, bf16[1,576,1024]{2,1,0:T(8,128)(2,1)S(1)} %copy-done.8, f32[576,4096]{1,0:T(8,128)} %get-tuple-element.93, f32[4096]{0:T(1024)} %bitcast.243), kind=kOutput, calls=%fused_computation.106 | convolution fusion | flops 4869582848 | bytes 33185792 | tf_op jit(solution)/shard_map/dot_general | solution.py:128
  357.4 10.7 %multiply_reduce_fusion.1 = (bf16[1024]{0:T(1024)(128)(2,1)}, f32[576]{0:T(1024)S(1)}, bf16[1024]{0:T(1024)(128)(2,1)}, f32[576,1024]{1,0:T(8,128)S(1)}) fusion(f32[576,1024]{1,0:T(8,128)S(1)} %get-tuple-element.92, f32[576]{0:T(1024)S(1)} %fusion.46, f32[576]{0:T(1024)S(1)} %broadcast_multiply_fusion, f32[1024]{0:T(1024)S(1)} %bitcast.237, ...), kind=kOutput, calls=%fused_computation.60 | convolution fusion | flops 4836554240 | bytes 17840896 | tf_op jit(solution)/shard_map/dot_general | solution.py:132
  374.6 11.8 %convolution_convert_fusion = bf16[1024,4096]{1,0:T(8,128)(2,1)} fusion(bf16[576,4096]{1,0:T(8,128)(2,1)} %copy-done.43, f32[576,1024]{1,0:T(8,128)S(1)} %get-tuple-element.92, f32[1024]{0:T(1024)S(1)} %bitcast.250, f32[1024]{0:T(1024)S(1)} %bitcast.239, f32[576]{0:T(1024)S(1)} %fusion.46, f32[576]{0:T(1024)S(1)} %broadcast_multiply_fusion), kind=kOutput, calls=%fused_computation.29 | convolution fusion | flops 4838981632 | bytes 15479296 | tf_op jit(solution)/shard_map/dot_general | solution.py:130
  411.9 11.9 %convolution_convert_fusion.1 = bf16[4096,1024]{1,0:T(8,128)(2,1)} fusion(bf16[576,4096]{1,0:T(8,128)(2,1)} %get-tuple-element.77, bf16[1,576,1024]{2,1,0:T(8,128)(2,1)S(1)} %copy-done.8), kind=kOutput, calls=%fused_computation.30 | convolution fusion | flops 4836032512 | bytes 14286848 | tf_op jit(solution)/shard_map/dot_general | solution.py:126
  439.5 19.3 %fusion.15 = bf16[8,64,1152]{2,1,0:T(8,128)(2,1)S(1)} fusion(bf16[1152,8,64]{0,2,1:T(8,128)(2,1)S(1)} %reshape.237, f32[8,1152,1152]{1,2,0:T(8,128)} %get-tuple-element.90, f32[8,1152]{1,0:T(8,128)} %log_add_fusion), kind=kOutput, calls=%fused_computation.38 | convolution fusion | flops 1380777984 | bytes 44863488 | tf_op jit(solution)/shard_map/while/body/eval_jaxpr/hqk,qhd->khd/dot_general | solution.py:68
  458.8 32.3 %multiply_reduce_fusion = (f32[8,1152]{1,0:T(8,128)}, f32[8,1152,1152]{1,2,0:T(8,128)}) fusion(f32[8,1152,1152]{1,2,0:T(8,128)} %get-tuple-element.90, f32[8,1152]{1,0:T(8,128)} %log_add_fusion, bf16[1152,8,64]{0,2,1:T(8,128)(2,1)S(1)} %reshape.237, bf16[1152,8,64]{0,2,1:T(8,128)(2,1)S(1)} %copy-done.16), kind=kOutput, calls=%fused_computation.3 | convolution fusion | flops 1390795776 | bytes 87367680 | tf_op jit(solution)/shard_map/while/body/eval_jaxpr/qhd,khd->hqk/dot_general | solution.py:57
  509.4 35.3 %multiply_convert_fusion = bf16[8,1152,1152]{1,2,0:T(8,128)(2,1)} fusion(f32[8,1152,1152]{1,2,0:T(8,128)} %get-tuple-element.96, f32[8,1152,1152]{1,2,0:T(8,128)} %get-tuple-element.90, f32[8,1152]{1,0:T(8,128)S(1)} %copy-done.24, f32[8,1152]{1,0:T(8,128)S(1)} %copy-done.17), kind=kLoop, calls=%fused_computation.2 | loop fusion | flops 42467328 | bytes 106242048 | tf_op jit(solution)/shard_map/while/body/eval_jaxpr/convert_element_type | solution.py:61
  544.7 10.7 %fusion.14 = bf16[8,64,1152]{2,1,0:T(8,128)(2,1)S(1)} fusion(bf16[1152,8,64]{0,2,1:T(8,128)(2,1)S(1)} %copy-done.5, bf16[8,1152,1152]{1,2,0:T(8,128)(2,1)} %multiply_convert_fusion), kind=kOutput, calls=%fused_computation.37 | convolution fusion | flops 1360134144 | bytes 23592960 | tf_op jit(solution)/shard_map/while/body/eval_jaxpr/hqk,qhd->khd/dot_general | solution.py:65
  573.5 11.2 %fusion.13 = bf16[8,64,1152]{2,1,0:T(8,128)(2,1)S(1)} fusion(bf16[1152,8,64]{0,2,1:T(8,128)(2,1)S(1)} %copy-done.7, bf16[8,1152,1152]{1,2,0:T(8,128)(2,1)} %multiply_convert_fusion), kind=kOutput, calls=%fused_computation.36 | convolution fusion | flops 1360134144 | bytes 23592960 | tf_op jit(solution)/shard_map/while/body/eval_jaxpr/hqk,khd->qhd/dot_general | solution.py:62
  661.2 10.3 %fusion.36 = bf16[1,576,1024]{2,1,0:T(8,128)(2,1)} fusion(f32[576,1024]{1,0:T(8,128)} %copy-done.9, bf16[576,4096]{1,0:T(8,128)(2,1)} %get-tuple-element.77, bf16[4096,1024]{1,0:T(8,128)(2,1)} %all-gather.15.cloned.1.call-done, f32[1024]{0:T(1024)} %bitcast.246), kind=kOutput, calls=%fused_computation.71 | convolution fusion | flops 4833607680 | bytes 16650240 | tf_op jit(solution)/shard_map/dot_general | solution.py:120
  671.4 30.8 %all-reduce = bf16[4096]{0:T(1024)(128)(2,1)} all-reduce(bf16[4096]{0:T(1024)(128)(2,1)} %get-tuple-element.98), channel_id=9, replica_groups=mesh['dp'=16,'seq'=2] {'dp'}, use_global_device_ids=true, to_apply=%region_32.33.clone | all-reduce | flops 4096 | bytes 16384
  711.6 58.1 %reduce-scatter.21.cloned.1.call-done = bf16[64,6]{1,0:T(8,128)(2,1)} async-done(((bf16[1024,6]{1,0:T(8,128)(2,1)}), bf16[64,6]{1,0:T(8,128)(2,1)}) %reduce-scatter.21.cloned.1.call-update) | async-done | bytes 784
  777.2 81.0 %reduce-scatter.11.cloned.1.call-done = bf16[64,3072]{1,0:T(8,128)(2,1)} async-done(((bf16[1024,3072]{1,0:T(8,128)(2,1)}), bf16[64,3072]{1,0:T(8,128)(2,1)}) %reduce-scatter.11.cloned.1.call-update) | async-done | bytes 393232 | tf_op jit(solution)/shard_map/reduce_scatter | solution.py:169
  858.3 15.1 %all-gather = bf16[128,3072]{1,0:T(8,128)(2,1)S(1)} all-gather(bf16[64,3072]{1,0:T(8,128)(2,1)} %reduce-scatter.11.cloned.1.call-done), channel_id=2, replica_groups=mesh['dp'=16,'seq'=2] {'seq'}, dimensions={0}, use_global_device_ids=true | all-gather | bytes 1179648 | tf_op jit(solution)/shard_map/all_gather | solution.py:192
  874.6 30.4 %all-reduce.5.cloned.1.call-done = (bf16[64,1024]{1,0:T(8,128)(2,1)}, bf16[64,4096]{1,0:T(8,128)(2,1)}, bf16[256,1024]{1,0:T(8,128)(2,1)}) async-done(((bf16[64,1024]{1,0:T(8,128)(2,1)}, bf16[64,4096]{1,0:T(8,128)(2,1)}, bf16[256,1024]{1,0:T(8,128)(2,1)}), (bf16[64,1024]{1,0:T(8,128)(2,1)}, bf16[64,4096]{1,0:T(8,128)(2,1)}, bf16[256,1024]{1,0:T(8,128)(2,1)})) %all-reduce.5.cloned.1.call-update) | async-done | bytes 1179664 | tf_op jit(solution)/shard_map/psum | solution.py:193
  (257 shorter events, 342.9 us)
Async XLA Ops:
  7.2 45.0 %copy-start.2 = (bf16[1,576,1024]{2,1,0:T(8,128)(2,1)S(1)}, bf16[1,576,1024]{2,1,0:T(8,128)(2,1)}, u32[]{:S(2)}) copy-start(bf16[1,576,1024]{2,1,0:T(8,128)(2,1)} %param.10) | copy-start | bytes 3538948
  7.2 67.7 %all-gather.9.cloned.1.call-start = ((), (), s32[]{:S(2)}) async-start(), calls=%async_computation.14 | async-start | bytes 6684672 | tf_op jit(solution)/shard_map/all_gather | solution.py:81
  7.9 299.1 %all-gather.11.cloned.1.call-start = ((), (), s32[]{:S(2)}) async-start(), calls=%async_computation.15 | async-start | bytes 2228224 | tf_op jit(solution)/shard_map/all_gather | solution.py:82
  8.7 302.2 %all-gather.13.cloned.1.call-start = ((), (), s32[]{:S(2)}) async-start(), calls=%async_computation.16 | async-start | bytes 8912896 | tf_op jit(solution)/shard_map/all_gather | solution.py:83
  101.3 23.0 %all-to-all-start.1 = ((bf16[2,2,147456]{2,1,0:T(2,128)(2,1)}), bf16[2,2,147456]{2,1,0:T(2,128)(2,1)}, u32[]{:S(2)}, u32[]{:S(2)}) async-start(bf16[2,2,147456]{2,1,0:T(2,128)(2,1)} %reshape.263), calls=%async_computation.1 | async-start | bytes 2359296 | tf_op jit(solution)/shard_map/all_to_all | solution.py:102
  124.3 21.5 %all-to-all-start.2 = ((bf16[2,2,147456]{2,1,0:T(2,128)(2,1)}), bf16[2,2,147456]{2,1,0:T(2,128)(2,1)}, u32[]{:S(2)}, u32[]{:S(2)}) async-start(bf16[2,2,147456]{2,1,0:T(2,128)(2,1)} %reshape.265), calls=%async_computation.2 | async-start | bytes 2359296 | tf_op jit(solution)/shard_map/all_to_all | solution.py:105
  145.8 41.7 %all-to-all-start = ((bf16[2,2,147456]{2,1,0:T(2,128)(2,1)}), bf16[2,2,147456]{2,1,0:T(2,128)(2,1)}, u32[]{:S(2)}, u32[]{:S(2)}) async-start(bf16[2,2,147456]{2,1,0:T(2,128)(2,1)} %reshape.261), calls=%async_computation | async-start | bytes 2359296 | tf_op jit(solution)/shard_map/all_to_all | solution.py:106
  150.3 191.4 %all-gather.15.cloned.1.call-start = ((), (), s32[]{:S(2)}) async-start(), calls=%async_computation.17 | async-start | bytes 8912896 | tf_op jit(solution)/shard_map/all_gather | solution.py:84
  169.3 39.5 %copy-start.4 = (bf16[1152,8,64]{0,2,1:T(8,128)(2,1)}, bf16[1152,8,64]{0,2,1:T(8,128)(2,1)S(1)}, u32[]{:S(2)}) copy-start(bf16[1152,8,64]{0,2,1:T(8,128)(2,1)S(1)} %reshape.230) | copy-start | bytes 3538948
  277.9 24.1 %all-to-all-start.3 = ((bf16[2,2,147456]{2,1,0:T(2,128)(2,1)}), bf16[2,2,147456]{2,1,0:T(2,128)(2,1)}, u32[]{:S(2)}, u32[]{:S(2)}) async-start(bf16[2,2,147456]{2,1,0:T(2,128)(2,1)} %reshape.267), calls=%async_computation.3 | async-start | bytes 2359296 | tf_op jit(solution)/shard_map/all_to_all | solution.py:109
  282.4 378.7 %reduce-scatter.13.cloned.1.call-start = ((), (), s32[]{:S(2)}) async-start(), calls=%async_computation.19 | async-start | bytes 2228224 | tf_op jit(solution)/shard_map/reduce_scatter | solution.py:172
  310.5 64.1 %copy-start.9 = (f32[576,1024]{1,0:T(8,128)}, f32[576,1024]{1,0:T(8,128)S(1)}, u32[]{:S(2)}) copy-start(f32[576,1024]{1,0:T(8,128)S(1)} %get-tuple-element.92) | copy-start | bytes 7077892
  374.6 286.5 %reduce-scatter.15.cloned.1.call-start = ((), (), s32[]{:S(2)}) async-start(), calls=%async_computation.20 | async-start | bytes 8912896 | tf_op jit(solution)/shard_map/reduce_scatter | solution.py:175
  407.4 20.5 %all-to-all-start.4 = ((bf16[2,2,147456]{2,1,0:T(2,128)(2,1)}), bf16[2,2,147456]{2,1,0:T(2,128)(2,1)}, u32[]{:S(2)}, u32[]{:S(2)}) async-start(bf16[2,2,147456]{2,1,0:T(2,128)(2,1)} %reshape.269), calls=%async_computation.4 | async-start | bytes 2359296 | tf_op jit(solution)/shard_map/all_to_all | solution.py:141
  411.8 249.3 %reduce-scatter.17.cloned.1.call-start = ((), (), s32[]{:S(2)}) async-start(), calls=%async_computation.21 | async-start | bytes 8912896 | tf_op jit(solution)/shard_map/reduce_scatter | solution.py:178
  504.9 64.1 %all-to-all-start.7 = ((bf16[2,2,147456]{2,1,0:T(2,128)(2,1)}), bf16[2,2,147456]{2,1,0:T(2,128)(2,1)}, u32[]{:S(2)}, u32[]{:S(2)}) async-start(bf16[2,2,147456]{2,1,0:T(2,128)(2,1)} %reshape.275), calls=%async_computation.7 | async-start | bytes 2359296 | tf_op jit(solution)/shard_map/all_to_all | solution.py:150
  569.0 29.3 %all-to-all-start.6 = ((bf16[2,2,147456]{2,1,0:T(2,128)(2,1)}), bf16[2,2,147456]{2,1,0:T(2,128)(2,1)}, u32[]{:S(2)}, u32[]{:S(2)}) async-start(bf16[2,2,147456]{2,1,0:T(2,128)(2,1)} %reshape.273), calls=%async_computation.6 | async-start | bytes 2359296 | tf_op jit(solution)/shard_map/all_to_all | solution.py:149
  598.3 19.8 %all-to-all-start.5 = ((bf16[2,2,147456]{2,1,0:T(2,128)(2,1)}), bf16[2,2,147456]{2,1,0:T(2,128)(2,1)S(1)}, u32[]{:S(2)}, u32[]{:S(2)}) async-start(bf16[2,2,147456]{2,1,0:T(2,128)(2,1)} %reshape.271), calls=%async_computation.5 | async-start | bytes 2359296 | tf_op jit(solution)/shard_map/all_to_all | solution.py:148
  601.9 108.8 %reduce-scatter.19.cloned.1.call-start = ((), (), s32[]{:S(2)}) async-start(), calls=%async_computation.22 | async-start | bytes 278528
  639.5 130.1 %reduce-scatter.21.cloned.1.call-start = ((), (), s32[]{:S(2)}) async-start(), calls=%async_computation.23 | async-start | bytes 278528
  649.5 208.8 %reduce-scatter.11.cloned.1.call-start = ((), (), s32[]{:S(2)}) async-start(), calls=%async_computation.18 | async-start | bytes 6684672 | tf_op jit(solution)/shard_map/reduce_scatter | solution.py:169
  659.2 245.8 %all-reduce.5.cloned.1.call-start = ((), (), s32[]{:S(2)}) async-start(), calls=%async_computation.24 | async-start | bytes 2359296 | tf_op jit(solution)/shard_map/psum | solution.py:193
  661.1 43.1 %copy-start.1 = (f32[576,1024]{1,0:T(8,128)S(1)}, f32[576,1024]{1,0:T(8,128)}, u32[]{:S(2)}) copy-start(f32[576,1024]{1,0:T(8,128)} %copy-done) | copy-start | bytes 7077892
  661.2 43.1 %copy-start.30 = (f32[576]{0:T(1024)S(1)}, f32[576]{0:T(1024)}, u32[]{:S(2)}) copy-start(f32[576]{0:T(1024)} %copy-done.29) | copy-start | bytes 6916
  (39 other events, 401.8 us)
Sparse Core Ops, SparseCore 0:
  10.3 64.5 all-gather.8
  77.1 40.0 all-gather.10
  119.4 73.6 all-gather.12
  195.1 73.2 all-gather.14
  374.7 59.2 reduce-scatter.12
  438.4 103.5 reduce-scatter.14
  546.7 104.3 reduce-scatter.16
  655.6 55.1 reduce-scatter.18
  715.3 54.3 reduce-scatter.20
  774.0 84.2 reduce-scatter.10
  860.7 44.1 all-reduce.4
